TPU v7x, 32 devices: a whole 2x2x4 slice. The times are simulated.
32 devices in a mesh: rep: 4 (over y, x), shard: 8 (over z, core).
Axes of the slice: x: 2, y: 2, z: 4, core: 2. Of those that a mesh axis runs over, the one named last changes fastest.
Arguments:
- tokens: bfloat16 [8192, 2048], P(('rep', 'shard')), may hold values from -6 to 6
- lengths: int32 [32], P(('rep', 'shard')), may hold values from 128 to 256, as said below
- routes: int32 [8192, 8], P(('rep', 'shard')), may hold values from 0 to 15, all different within a row; in each aligned block of 256 rows (0 to 255, 256 to 511, ...) at most 144 rows name the same one
- gain_attn: float32 [2048], replicated, may hold values from 0.1 to 1.9
- gain_query: float32 [128], replicated, may hold values from 0.1 to 1.9
- gain_key: float32 [128], replicated, may hold values from 0.1 to 1.9
- w_query: bfloat16 [2048, 2048], P(None, 'shard'), may hold values from -0.125 to 0.125
- w_key: bfloat16 [2048, 2048], P(None, 'shard'), may hold values from -0.125 to 0.125
- w_value: bfloat16 [2048, 2048], P(None, 'shard'), may hold values from -0.125 to 0.125
- w_out: bfloat16 [2048, 2048], P('shard'), may hold values from -0.75 to 0.75
- gain_moe: float32 [2048], replicated, may hold values from 0.1 to 1.9
- w_router: bfloat16 [2048, 16], replicated, may hold values from -0.0625 to 0.0625
- w_gate: bfloat16 [16, 2048, 1024], P('shard'), may hold values from -0.125 to 0.125
- w_up: bfloat16 [16, 2048, 1024], P('shard'), may hold values from -0.125 to 0.125
- w_down: bfloat16 [16, 1024, 2048], P('shard'), may hold values from -1.5 to 1.5
- out_grad: bfloat16 [8192, 2048], P(('rep', 'shard')), may hold values from -6 to 6
Outputs:
- output: bfloat16 [8192, 2048], P(('rep', 'shard'))
- input_grad: float32 [8192, 2048], P(('rep', 'shard'))
- grad_gain_attn: float32 [2048], replicated
- grad_gain_query: float32 [128], replicated
- grad_gain_key: float32 [128], replicated
- grad_w_query: float32 [2048, 2048], P(None, 'shard')
- grad_w_key: float32 [2048, 2048], P(None, 'shard')
- grad_w_value: float32 [2048, 2048], P(None, 'shard')
- grad_w_out: float32 [2048, 2048], P('shard')
- grad_gain_moe: float32 [2048], replicated
- grad_w_router: float32 [2048, 16], replicated
- grad_w_gate: float32 [16, 2048, 1024], P('shard')
- grad_w_up: float32 [16, 2048, 1024], P('shard')
- grad_w_down: float32 [16, 1024, 2048], P('shard')
Inputs may be any that keep to these rules, and one draw needn't show every extreme that they name: `lengths`: valid tokens of each sequence; some sequence is full. `routes`: each row names 8 different experts; among the 256 rows of one sequence no expert is named by more than 144 rows, a bound that some block reaches.
All inputs are finite; a program needn't handle non-finite values.
Results may differ from a plain program's by a relative error of at most 0.024.
Values may be sent and summed in bfloat16 or wider, within the bound.
A program may use at most 320 MiB of HBM per device.

v0:
```python
import jax
import jax.numpy as jnp
from jax import lax
from jax.sharding import PartitionSpec as P

CAP = 144
EPS_NORM = 1e-06
ROPE_BASE = 50000.0
MASKED = -1e30


def rms_scale(values, gain_vec):
    return (
        values * lax.rsqrt(jnp.mean(values * values, axis=-1, keepdims=True) + EPS_NORM) * gain_vec
    )


def rope_tables(seq_len, head_dim):
    half_dim = head_dim // 2
    places = jnp.arange(seq_len, dtype=jnp.float32)
    freqs = ROPE_BASE ** (-jnp.arange(half_dim, dtype=jnp.float32) * (2.0 / head_dim))
    angles = places[:, None] * freqs[None, :]
    cos_tab = jnp.concatenate([jnp.cos(angles), jnp.cos(angles)], axis=-1)
    sine_tab = jnp.concatenate([jnp.sin(angles), jnp.sin(angles)], axis=-1)
    return (cos_tab, sine_tab)


def rotate_half(values, cos_tab, sine_tab):
    half_dim = values.shape[-1] // 2
    turned = jnp.concatenate([-values[..., half_dim:], values[..., :half_dim]], axis=-1)
    return values * cos_tab[:, None, :] + turned * sine_tab[:, None, :]


def head_prepare(raw_proj, gain_vec, cos_tab, sine_tab):
    return rotate_half(rms_scale(raw_proj, gain_vec), cos_tab, sine_tab)


def soft_max(logit_vals):
    upper = jnp.max(logit_vals, axis=-1, keepdims=True)
    expo = jnp.exp(logit_vals - upper)
    return expo / jnp.sum(expo, axis=-1, keepdims=True)


def slot_table(route_rows, expert_count):
    flat_ids = route_rows.reshape(-1)
    one_hot = (flat_ids[:, None] == jnp.arange(expert_count, dtype=jnp.int32)[None, :]).astype(
        jnp.int32
    )
    before = jnp.cumsum(one_hot, axis=0) - one_hot
    ranks = jnp.sum(before * one_hot, axis=1)
    return flat_ids * CAP + ranks


def attend(query_rot, key_rot, value_low, key_valid, score_scale):
    scores = (
        jnp.einsum("sqhd,skhd->shqk", query_rot, key_rot, preferred_element_type=jnp.float32)
        * score_scale
    )
    scores = jnp.where(key_valid[:, None, None, :], scores, MASKED)
    upper = jnp.max(scores, axis=-1, keepdims=True)
    expo = jnp.exp(scores - upper)
    total = jnp.sum(expo, axis=-1, keepdims=True)
    weights = (expo / total).astype(jnp.bfloat16)
    result = jnp.einsum("shqk,skhd->sqhd", weights, value_low, preferred_element_type=jnp.float32)
    return (result.astype(jnp.bfloat16), upper + jnp.log(total))


def attend_back(query_rot, key_rot, value_low, key_valid, score_scale, log_total, grad_result):
    scores = (
        jnp.einsum("sqhd,skhd->shqk", query_rot, key_rot, preferred_element_type=jnp.float32)
        * score_scale
    )
    scores = jnp.where(key_valid[:, None, None, :], scores, MASKED)
    probs_full = jnp.exp(scores - log_total)
    weights = probs_full.astype(jnp.bfloat16)
    grad_value = jnp.einsum(
        "shqk,sqhd->skhd", weights, grad_result, preferred_element_type=jnp.float32
    ).astype(jnp.bfloat16)
    grad_prob = jnp.einsum(
        "sqhd,skhd->shqk", grad_result, value_low, preferred_element_type=jnp.float32
    )
    mean_term = jnp.sum(probs_full * grad_prob, axis=-1, keepdims=True)
    grad_score = (probs_full * (grad_prob - mean_term)).astype(jnp.bfloat16)
    grad_query = (
        jnp.einsum("shqk,skhd->sqhd", grad_score, key_rot, preferred_element_type=jnp.float32)
        * score_scale
    )
    grad_key = (
        jnp.einsum("shqk,sqhd->skhd", grad_score, query_rot, preferred_element_type=jnp.float32)
        * score_scale
    )
    return (grad_query, grad_key, grad_value)


def local(
    tokens,
    lengths,
    routes,
    gain_attn,
    gain_query,
    gain_key,
    w_query,
    w_key,
    w_value,
    w_out,
    gain_moe,
    w_router,
    w_gate,
    w_up,
    w_down,
    out_grad,
):
    row_count, model_width = tokens.shape
    head_dim = gain_query.shape[0]
    group_count = lax.axis_size("shard")
    expert_count = w_router.shape[1]
    inputs = tokens.astype(jnp.float32)
    row_valid = jnp.arange(row_count, dtype=jnp.int32) < lengths[0]
    row_mask = row_valid.astype(jnp.float32)
    cos_tab, sine_tab = rope_tables(row_count, head_dim)
    score_scale = head_dim ** (-0.5)
    normed_low = rms_scale(inputs, gain_attn).astype(jnp.bfloat16)
    source, key_marks = (
        lax.all_gather(normed_low, "shard", axis=0, tiled=True),
        lax.all_gather(row_mask.astype(jnp.bfloat16), "shard", axis=0, tiled=True),
    )
    key_valid = key_marks.reshape(group_count, row_count) > 0.5
    proj_query, proj_key, proj_value, proj_out = (w_query, w_key, w_value, w_out)
    head_local = proj_query.shape[1] // head_dim
    four_shape = (group_count, row_count, head_local, head_dim)
    flat_shape = (group_count * row_count, head_local * head_dim)
    query_raw = jnp.dot(source, proj_query, preferred_element_type=jnp.float32).reshape(four_shape)
    key_raw = jnp.dot(source, proj_key, preferred_element_type=jnp.float32).reshape(four_shape)
    value_low = jnp.dot(source, proj_value, preferred_element_type=jnp.float32).astype(jnp.bfloat16)
    value_low = value_low.reshape(four_shape)
    query_rot = head_prepare(query_raw, gain_query, cos_tab, sine_tab).astype(jnp.bfloat16)
    key_rot = head_prepare(key_raw, gain_key, cos_tab, sine_tab).astype(jnp.bfloat16)
    attended, log_total = attend(query_rot, key_rot, value_low, key_valid, score_scale)
    flat_attended = attended.reshape(flat_shape)
    branch = lax.psum_scatter(
        jnp.dot(flat_attended, proj_out, preferred_element_type=jnp.float32),
        "shard",
        scatter_dimension=0,
        tiled=True,
    )
    hidden = inputs + branch
    moe_low = rms_scale(hidden, gain_moe).astype(jnp.bfloat16)
    router_probs = soft_max(jnp.dot(moe_low, w_router, preferred_element_type=jnp.float32))
    route_hot = (
        routes[:, :, None] == jnp.arange(expert_count, dtype=jnp.int32)[None, None, :]
    ).astype(jnp.float32)
    gate_vals = jnp.sum(router_probs[:, None, :] * route_hot, axis=-1)
    slot_ids = slot_table(routes, expert_count)
    copies = jnp.repeat(moe_low, routes.shape[1], axis=0)
    send_rows = jnp.zeros((expert_count * CAP, model_width), jnp.bfloat16).at[slot_ids].set(copies)
    arrived = lax.all_to_all(
        send_rows.reshape(expert_count, CAP, model_width),
        "shard",
        split_axis=0,
        concat_axis=1,
        tiled=True,
    )
    gate_act = jnp.einsum("erd,edf->erf", arrived, w_gate, preferred_element_type=jnp.float32)
    up_act = jnp.einsum("erd,edf->erf", arrived, w_up, preferred_element_type=jnp.float32)
    sig_gate = jax.nn.sigmoid(gate_act)
    silu_gate = gate_act * sig_gate
    joined = (silu_gate * up_act).astype(jnp.bfloat16)
    expert_out = jnp.einsum(
        "erf,efd->erd", joined, w_down, preferred_element_type=jnp.float32
    ).astype(jnp.bfloat16)
    returned = lax.all_to_all(expert_out, "shard", split_axis=1, concat_axis=0, tiled=True).reshape(
        expert_count * CAP, model_width
    )
    picked = returned[slot_ids].astype(jnp.float32).reshape(row_count, -1, model_width)
    mixture = jnp.sum(picked * gate_vals[:, :, None], axis=1)
    output = (hidden + mixture).astype(jnp.bfloat16)
    grad_out = out_grad.astype(jnp.float32) * row_mask[:, None]
    grad_gates = jnp.sum(picked * grad_out[:, None, :], axis=-1)
    grad_rows = (
        (gate_vals[:, :, None] * grad_out[:, None, :]).astype(jnp.bfloat16).reshape(-1, model_width)
    )
    grad_send = (
        jnp.zeros((expert_count * CAP, model_width), jnp.bfloat16).at[slot_ids].set(grad_rows)
    )
    grad_arrived = lax.all_to_all(
        grad_send.reshape(expert_count, CAP, model_width),
        "shard",
        split_axis=0,
        concat_axis=1,
        tiled=True,
    )
    grad_joined = jnp.einsum(
        "erd,efd->erf", grad_arrived, w_down, preferred_element_type=jnp.float32
    )
    grad_down = jnp.einsum("erf,erd->efd", joined, grad_arrived, preferred_element_type=jnp.float32)
    grad_gate_act = (grad_joined * up_act * sig_gate * (1.0 + gate_act * (1.0 - sig_gate))).astype(
        jnp.bfloat16
    )
    grad_up_act = (grad_joined * silu_gate).astype(jnp.bfloat16)
    grad_expert_in = jnp.einsum(
        "erf,edf->erd", grad_gate_act, w_gate, preferred_element_type=jnp.float32
    ) + jnp.einsum("erf,edf->erd", grad_up_act, w_up, preferred_element_type=jnp.float32)
    grad_expert_in = grad_expert_in.astype(jnp.bfloat16)
    grad_gate_w = jnp.einsum(
        "erd,erf->edf", arrived, grad_gate_act, preferred_element_type=jnp.float32
    )
    grad_up_w = jnp.einsum("erd,erf->edf", arrived, grad_up_act, preferred_element_type=jnp.float32)
    grad_back = lax.all_to_all(
        grad_expert_in, "shard", split_axis=1, concat_axis=0, tiled=True
    ).reshape(expert_count * CAP, model_width)
    grad_moe_in = jnp.sum(
        grad_back[slot_ids].astype(jnp.float32).reshape(row_count, -1, model_width), axis=1
    )
    grad_probs = jnp.sum(grad_gates[:, :, None] * route_hot, axis=1)
    grad_logits = router_probs * (
        grad_probs - jnp.sum(router_probs * grad_probs, axis=-1, keepdims=True)
    )
    router_full = w_router.astype(jnp.float32)
    grad_moe_in = grad_moe_in + jnp.dot(grad_logits, router_full.T, precision=lax.Precision.HIGHEST)
    grad_router = jnp.dot(
        moe_low.astype(jnp.float32).T, grad_logits, precision=lax.Precision.HIGHEST
    )
    moe_unused, pull_moe = jax.vjp(rms_scale, hidden, gain_moe)
    grad_hidden_part, grad_gain_moe = pull_moe(grad_moe_in)
    grad_hidden = grad_out + grad_hidden_part
    grad_branch = grad_hidden.astype(jnp.bfloat16)
    branch_rows = lax.all_gather(grad_branch, "shard", axis=0, tiled=True)
    grad_attended = jnp.dot(branch_rows, proj_out.T, preferred_element_type=jnp.float32).astype(
        jnp.bfloat16
    )
    grad_out_w = jnp.dot(flat_attended.T, branch_rows, preferred_element_type=jnp.float32)
    grad_query_rot, grad_key_rot, grad_value = attend_back(
        query_rot,
        key_rot,
        value_low,
        key_valid,
        score_scale,
        log_total,
        grad_attended.reshape(four_shape),
    )

    def prepare(raw_proj, gain_vec):
        return head_prepare(raw_proj, gain_vec, cos_tab, sine_tab)

    query_unused, pull_query = jax.vjp(prepare, query_raw, gain_query)
    grad_query_raw, grad_gain_query = pull_query(grad_query_rot)
    key_unused, pull_key = jax.vjp(prepare, key_raw, gain_key)
    grad_key_raw, grad_gain_key = pull_key(grad_key_rot)
    grad_q_low = grad_query_raw.astype(jnp.bfloat16).reshape(flat_shape)
    grad_k_low = grad_key_raw.astype(jnp.bfloat16).reshape(flat_shape)
    grad_v_low = grad_value.reshape(flat_shape)
    grad_query_w = jnp.dot(source.T, grad_q_low, preferred_element_type=jnp.float32)
    grad_key_w = jnp.dot(source.T, grad_k_low, preferred_element_type=jnp.float32)
    grad_value_w = jnp.dot(source.T, grad_v_low, preferred_element_type=jnp.float32)
    grad_normed = lax.psum_scatter(
        (
            jnp.dot(grad_q_low, proj_query.T, preferred_element_type=jnp.float32)
            + jnp.dot(grad_k_low, proj_key.T, preferred_element_type=jnp.float32)
            + jnp.dot(grad_v_low, proj_value.T, preferred_element_type=jnp.float32)
        ).astype(jnp.bfloat16),
        "shard",
        scatter_dimension=0,
        tiled=True,
    ).astype(jnp.float32)
    attn_unused, pull_attn = jax.vjp(rms_scale, inputs, gain_attn)
    grad_input_part, grad_gain_attn = pull_attn(grad_normed)
    grad_input = grad_hidden + grad_input_part
    summed = (
        lax.psum(grad_query_w.astype(jnp.bfloat16), "rep").astype(jnp.float32),
        lax.psum(grad_key_w.astype(jnp.bfloat16), "rep").astype(jnp.float32),
        lax.psum(grad_value_w.astype(jnp.bfloat16), "rep").astype(jnp.float32),
        lax.psum(grad_out_w.astype(jnp.bfloat16), "rep").astype(jnp.float32),
        lax.psum(grad_gate_w.astype(jnp.bfloat16), "rep").astype(jnp.float32),
        lax.psum(grad_up_w.astype(jnp.bfloat16), "rep").astype(jnp.float32),
        lax.psum(grad_down.astype(jnp.bfloat16), "rep").astype(jnp.float32),
    )
    shared = lax.psum(
        (grad_gain_attn, grad_gain_query, grad_gain_key, grad_gain_moe, grad_router),
        ("rep", "shard"),
    )
    return (
        output,
        grad_input,
        shared[0],
        shared[1],
        shared[2],
        summed[0],
        summed[1],
        summed[2],
        summed[3],
        shared[3],
        shared[4],
        summed[4],
        summed[5],
        summed[6],
    )


def solution(mesh):
    return jax.shard_map(
        local,
        mesh=mesh,
        in_specs=(
            P(("rep", "shard"), None),
            P(("rep", "shard")),
            P(("rep", "shard"), None),
            P(),
            P(),
            P(),
            P(None, "shard"),
            P(None, "shard"),
            P(None, "shard"),
            P("shard", None),
            P(),
            P(),
            P("shard", None, None),
            P("shard", None, None),
            P("shard", None, None),
            P(("rep", "shard"), None),
        ),
        out_specs=(
            P(("rep", "shard"), None),
            P(("rep", "shard"), None),
            P(),
            P(),
            P(),
            P(None, "shard"),
            P(None, "shard"),
            P(None, "shard"),
            P("shard", None),
            P(),
            P(),
            P("shard", None, None),
            P("shard", None, None),
            P("shard", None, None),
        ),
        check_vma=False,
    )
```

profile of v0, /device:TPU:0, one launch (start us, length us, event | category | flops | bytes accessed | tf_op | source)
XLA Modules:
  0.0 2252.7 jit_solution(6892973722710807610)
XLA Ops:
  28.4 69.1 %all-gather.4.cloned.1.call-done = bf16[2048,2048]{1,0:T(8,128)(2,1)} async-done(((bf16[256,2048]{1,0:T(8,128)(2,1)}), bf16[2048,2048]{1,0:T(8,128)(2,1)}) %all-gather.4.cloned.1.call-update) | async-done | bytes 8388624 | tf_op jit(solution)/shard_map/all_gather | solution.py:124
  174.2 158.8 %reduce-scatter.3.cloned.1.call-done = f32[256,2048]{1,0:T(8,128)} async-done(((f32[2048,2048]{1,0:T(8,128)}), f32[256,2048]{1,0:T(8,128)}) %reduce-scatter.3.cloned.1.call-update) | async-done | bytes 2097168 | tf_op jit(solution)/shard_map/reduce_scatter | solution.py:140
  339.4 18.5 scatter_custom_fusion.1
  363.4 17.6 scatter_custom_fusion
  381.0 188.8 %all-to-all-done.2 = bf16[16,144,2048]{2,1,0:T(8,128)(2,1)} async-done(((bf16[16,144,2048]{2,1,0:T(8,128)(2,1)}), bf16[16,144,2048]{2,1,0:T(8,128)(2,1)}, u32[]{:S(2)}, u32[]{:S(2)}) %all-to-all-start.2) | async-done | bytes 9437216 | tf_op jit(solution)/shard_map/all_to_all | solution.py:185
  584.3 197.1 %all-to-all-done = bf16[16,144,2048]{2,1,0:T(8,128)(2,1)} async-done(((bf16[16,144,2048]{2,1,0:T(8,128)(2,1)}), bf16[16,144,2048]{2,1,0:T(8,128)(2,1)}, u32[]{:S(2)}, u32[]{:S(2)}) %all-to-all-start) | async-done | bytes 9437216 | tf_op jit(solution)/shard_map/all_to_all | solution.py:156
  790.8 17.2 fusion.76
  822.5 23.1 %multiply_convert_fusion = (bf16[2,1152,1024]{2,1,0:T(8,128)(2,1)}, bf16[2,1152,1024]{2,1,0:T(8,128)(2,1)}, bf16[2,1152,1024]{2,1,0:T(8,128)(2,1)}) fusion(f32[2,1152,1024]{2,1,0:T(8,128)} %fusion.75, f32[2,1152,1024]{2,1,0:T(8,128)} %fusion.76, bf16[2,1152,2048]{2,1,0:T(8,128)(2,1)} %bitcast.161, bf16[2,1024,2048]{2,1,0:T(8,128)(2,1)} %param.30), kind=kOutput, calls=%fused_computation.14 | convolution fusion | flops 9699065856 | bytes 50855936 | tf_op jit(solution)/shard_map/erd,efd->erf/dot_general | solution.py:192
  859.9 27.9 %copy.302 = bf16[2,1152,2048]{2,0,1:T(2,128)(2,1)} copy(bf16[2,1152,2048]{2,1,0:T(8,128)(2,1)S(1)} %convolution_convert_fusion) | data formatting | bytes 18874368 | tf_op jit(solution)/shard_map/convert_element_type | solution.py:170
  893.1 17.5 fusion.77
  910.6 18.6 add_convert_fusion
  929.2 18.2 copy.307
  947.4 152.0 %all-to-all-done.1 = bf16[2,1152,2048]{2,0,1:T(2,128)(2,1)} async-done(((bf16[2,1152,2048]{2,0,1:T(2,128)(2,1)}), bf16[2,1152,2048]{2,0,1:T(2,128)(2,1)}, u32[]{:S(2)}, u32[]{:S(2)}) %all-to-all-start.1) | async-done | bytes 9437216 | tf_op jit(solution)/shard_map/all_to_all | solution.py:171
  1116.7 21.6 gather_fusion
  1148.0 162.9 %all-to-all-done.3 = bf16[2,1152,2048]{2,0,1:T(2,128)(2,1)} async-done(((bf16[2,1152,2048]{2,0,1:T(2,128)(2,1)}), bf16[2,1152,2048]{2,0,1:T(2,128)(2,1)}, u32[]{:S(2)}, u32[]{:S(2)}) %all-to-all-start.3) | async-done | bytes 9437216 | tf_op jit(solution)/shard_map/all_to_all | solution.py:208
  1322.7 21.6 gather_fusion.1
  1362.9 80.9 %all-gather.6.cloned.1.call-done = bf16[2048,2048]{1,0:T(8,128)(2,1)} async-done(((bf16[256,2048]{1,0:T(8,128)(2,1)}), bf16[2048,2048]{1,0:T(8,128)(2,1)}) %all-gather.6.cloned.1.call-update) | async-done | bytes 8388624 | tf_op jit(solution)/shard_map/all_gather | solution.py:227
  1487.5 15.6 add_convert_fusion.1
  1503.2 18.8 convolution_convert_fusion.1
  1522.0 17.2 convolution_convert_fusion.2
  1539.3 15.7 convolution_convert_fusion.3
  1597.5 38.8 %all-reduce.4 = (f32[2048]{0:T(1024)}, f32[128]{0:T(128)}, f32[128]{0:T(128)}, f32[2048]{0:T(1024)}) all-reduce(f32[2048]{0:T(1024)S(1)} %get-tuple-element.22, f32[128]{0:T(128)S(1)} %get-tuple-element.56, f32[128]{0:T(128)S(1)} %get-tuple-element.18, f32[2048]{0:T(1024)S(1)} %copy-done.65), channel_id=1, replica_groups=mesh['rep'=4,'shard'=8] {'rep','shard'}, use_global_device_ids=true, to_apply=%region_27.28 | all-reduce | flops 4352 | bytes 34816 | tf_op jit(solution)/shard_map/psum | solution.py:277
  1636.3 478.5 %all-reduce.11.cloned.1.call-done = (bf16[2048,256]{1,0:T(8,128)(2,1)}, bf16[2048,256]{1,0:T(8,128)(2,1)}, bf16[2048,256]{1,0:T(8,128)(2,1)}, bf16[256,2048]{1,0...) async-done(((bf16[2048,256]{1,0:T(8,128)(2,1)}, bf16[2048,256]{1,0:T(8,128)(2,1)}, ...) | async-done | bytes 29360144 | tf_op jit(solution)/shard_map/psum | solution.py:269
  2158.5 85.6 %all-reduce.9.cloned.1.call-done = f32[2048,16]{0,1:T(8,128)} async-done(((f32[2048,16]{0,1:T(8,128)}), f32[2048,16]{0,1:T(8,128)}) %all-reduce.9.cloned.1.call-update) | async-done | bytes 131088 | tf_op jit(solution)/shard_map/psum | solution.py:277
  (323 shorter events, 354.6 us)
Async XLA Ops:
  7.2 150.2 %copy-start = (bf16[256,2048]{1,0:T(8,128)(2,1)S(1)}, bf16[256,2048]{1,0:T(8,128)(2,1)}, u32[]{:S(2)}) copy-start(bf16[256,2048]{1,0:T(8,128)(2,1)} %param.25) | copy-start | bytes 3145732
  7.2 90.3 %copy-start.33 = (bf16[2048,256]{1,0:T(8,128)(2,1)S(1)}, bf16[2048,256]{1,0:T(8,128)(2,1)}, u32[]{:S(2)}) copy-start(bf16[2048,256]{1,0:T(8,128)(2,1)} %param.23) | copy-start | bytes 3145732
  7.2 90.3 %all-gather.4.cloned.1.call-start = ((), (), s32[]{:S(2)}) async-start(), calls=%async_computation.6 | async-start | bytes 9437184 | tf_op jit(solution)/shard_map/all_gather | solution.py:124
  12.6 320.3 %reduce-scatter.3.cloned.1.call-start = ((), (), s32[]{:S(2)}) async-start(), calls=%async_computation.7 | async-start | bytes 18874368 | tf_op jit(solution)/shard_map/reduce_scatter | solution.py:140
  114.5 33.7 %copy-start.3 = (f32[8,256,2,128]{1,3,2,0:T(8,128)}, f32[8,256,2,128]{1,3,2,0:T(8,128)S(1)}, u32[]{:S(2)}) copy-start(f32[8,256,2,128]{1,3,2,0:T(8,128)S(1)} %copy.292) | copy-start | bytes 6291460
  166.6 166.3 %copy-start.8 = (bf16[256,2048]{1,0:T(8,128)(2,1)S(1)}, bf16[256,2048]{1,0:T(8,128)(2,1)}, u32[]{:S(2)}) copy-start(bf16[256,2048]{1,0:T(8,128)(2,1)} %param.16) | copy-start | bytes 3145732
  172.4 162.5 %copy-start.86 = (f32[256]{0:T(256)}, f32[256]{0:T(256)S(1)}, u32[]{:S(2)}) copy-start(f32[256]{0:T(256)S(1)} %compare_convert_fusion) | copy-start | bytes 3076
  172.6 190.8 %copy-start.66 = (s32[2048,1]{0,1:T(1,128)}, s32[2048,1]{0,1:T(1,128)S(1)}, u32[]{:S(2)}) copy-start(s32[2048,1]{0,1:T(1,128)S(1)} %compare_select_fusion) | copy-start | bytes 24580
  172.6 163.6 %copy-start.61 = (f32[2048]{0:T(1024)S(1)}, f32[2048]{0:T(1024)}, u32[]{:S(2)}) copy-start(f32[2048]{0:T(1024)} %param.26) | copy-start | bytes 24580
  174.2 163.3 %copy-start.39 = (bf16[2048,16]{0,1:T(8,128)(2,1)S(1)}, bf16[2048,16]{0,1:T(8,128)(2,1)}, u32[]{:S(2)}) copy-start(bf16[2048,16]{0,1:T(8,128)(2,1)} %param.27) | copy-start | bytes 196612
  358.0 211.7 %all-to-all-start.2 = ((bf16[16,144,2048]{2,1,0:T(8,128)(2,1)}), bf16[16,144,2048]{2,1,0:T(8,128)(2,1)}, u32[]{:S(2)}, u32[]{:S(2)}) async-start(bf16[16,144,2048]{2,1,0:T(8,128)(2,1)} %bitcast.160), calls=%async_computation.3 | async-start | bytes 18874368 | tf_op jit(solution)/shard_map/all_to_all | solution.py:185
  569.7 211.7 %all-to-all-start = ((bf16[16,144,2048]{2,1,0:T(8,128)(2,1)}), bf16[16,144,2048]{2,1,0:T(8,128)(2,1)}, u32[]{:S(2)}, u32[]{:S(2)}) async-start(bf16[16,144,2048]{2,1,0:T(8,128)(2,1)} %bitcast.159), calls=%async_computation.1 | async-start | bytes 18874368 | tf_op jit(solution)/shard_map/all_to_all | solution.py:156
  887.8 211.7 %all-to-all-start.1 = ((bf16[2,1152,2048]{2,0,1:T(2,128)(2,1)}), bf16[2,1152,2048]{2,0,1:T(2,128)(2,1)}, u32[]{:S(2)}, u32[]{:S(2)}) async-start(bf16[2,1152,2048]{2,0,1:T(2,128)(2,1)} %copy.302), calls=%async_computation.2 | async-start | bytes 18874368 | tf_op jit(solution)/shard_map/all_to_all | solution.py:171
  947.4 157.4 %copy-start.67 = (s32[2048,1]{0,1:T(1,128)S(1)}, s32[2048,1]{0,1:T(1,128)}, u32[]{:S(2)}) copy-start(s32[2048,1]{0,1:T(1,128)} %copy-done.66) | copy-start | bytes 24580
  1099.4 211.4 %all-to-all-start.3 = ((bf16[2,1152,2048]{2,0,1:T(2,128)(2,1)}), bf16[2,1152,2048]{2,0,1:T(2,128)(2,1)}, u32[]{:S(2)}, u32[]{:S(2)}) async-start(bf16[2,1152,2048]{2,0,1:T(2,128)(2,1)} %copy.307), calls=%async_computation.4 | async-start | bytes 18874368 | tf_op jit(solution)/shard_map/all_to_all | solution.py:208
  1104.5 339.3 %all-gather.6.cloned.1.call-start = ((), (), s32[]{:S(2)}) async-start(), calls=%async_computation.8 | async-start | bytes 9437184 | tf_op jit(solution)/shard_map/all_gather | solution.py:227
  1116.7 21.7 copy-start.31
  1147.9 207.9 %copy-start.44 = (f32[256,16]{0,1:T(8,128)}, f32[256,16]{0,1:T(8,128)S(1)}, u32[]{:S(2)}) copy-start(f32[256,16]{0,1:T(8,128)S(1)} %select_reduce_fusion) | copy-start | bytes 49156
  1148.0 207.9 %copy-start.78 = (f32[256]{0:T(256)}, f32[256]{0:T(256)S(1)}, u32[]{:S(2)}) copy-start(f32[256]{0:T(256)S(1)} %multiply_reduce_fusion.10) | copy-start | bytes 3076
  1362.9 228.6 %reduce-scatter.5.cloned.1.call-start = ((), (), s32[]{:S(2)}) async-start(), calls=%async_computation.9 | async-start | bytes 9437184 | tf_op jit(solution)/shard_map/reduce_scatter | solution.py:255
  1503.1 611.6 %all-reduce.11.cloned.1.call-start = ((), (), s32[]{:S(2)}) async-start(), calls=%async_computation.11 | async-start | bytes 58720256 | tf_op jit(solution)/shard_map/psum | solution.py:269
  1503.2 36.1 %slice-start = ((s8[9437184]{0:T(1024)(128)(4,1)}), s8[4194304]{0:T(1024)(128)(4,1)S(1)}, s32[]{:S(2)}) async-start(s8[9437184]{0:T(1024)(128)(4,1)} %bitcast.166), calls=%async_computation.12 | async-start | bytes 8388608
  1503.2 36.1 %slice-start.1 = ((s8[9437184]{0:T(1024)(128)(4,1)}), s8[4194304]{0:T(1024)(128)(4,1)S(1)}, s32[]{:S(2)}) async-start(s8[9437184]{0:T(1024)(128)(4,1)} %bitcast.166), calls=%async_computation.13 | async-start | bytes 8388608
  1579.7 664.4 %all-reduce.9.cloned.1.call-start = ((), (), s32[]{:S(2)}) async-start(), calls=%async_computation.10 | async-start | bytes 262144 | tf_op jit(solution)/shard_map/psum | solution.py:277
  (79 other events, 435.2 us)
Sparse Core Ops, SparseCore 0:
  12.7 84.7 all-gather.3
  166.1 166.8 reduce-scatter.2
  1363.0 80.8 all-gather.5
  1503.2 88.1 reduce-scatter.4
  1597.1 517.5 all-reduce.10
  2121.6 122.3 all-reduce.8
where the time goes:
time: 2260 us; the launch traced here: 2250 us
  waiting for transfers between devices  1580 us (70%)
  matrix products  264 us (12%)
  local copies, waits for them, and re-layouts  191 us (8%)
  other arithmetic  124 us (5%)
  blocking collectives  52.2 us (2%)
    psum x1, waiting for transfers between devices, local(): lax.psum(grad_query_w.astype(jnp.bfloat16), 'rep').astype(jnp.float32)  478 us
    all_to_all x1, waiting for transfers between devices, local(): lax.all_to_all(send_rows.reshape(expert_count, CAP, model_width), 'shard'...  197 us
    all_to_all x1, waiting for transfers between devices, local(): lax.all_to_all(grad_send.reshape(expert_count, CAP, model_width), 'shard'...  189 us
    all_to_all x1, waiting for transfers between devices, local(): lax.all_to_all(grad_expert_in, 'shard', split_axis=1, concat_axis=0, tile...  163 us
    reduce_scatter x1, waiting for transfers between devices, local(): lax.psum_scatter(jnp.dot(flat_attended, proj_out, preferred_element_type=...  159 us
    all_to_all x1, waiting for transfers between devices, local(): lax.all_to_all(expert_out, 'shard', split_axis=1, concat_axis=0, tiled=True)  152 us
    psum x1, waiting for transfers between devices, local(): lax.psum((grad_gain_attn, grad_gain_query, grad_gain_key, grad_gain_moe,...  85.6 us
    all_gather x1, waiting for transfers between devices, local(): branch_rows = lax.all_gather(grad_branch, 'shard', axis=0, tiled=True)  80.9 us
  transfers between devices with their start and end apart: 10, of which 10 were waited for; matrix products, arithmetic and copies ran while one was open for 12% of the time, Pallas kernels for 0%

commit v1 on v0

--- a/solution.py
+++ b/solution.py
@@ -275,8 +275,10 @@
         lax.psum(grad_down.astype(jnp.bfloat16), "rep").astype(jnp.float32),
     )
     shared = lax.psum(
-        (grad_gain_attn, grad_gain_query, grad_gain_key, grad_gain_moe, grad_router),
-        ("rep", "shard"),
+        lax.psum(
+            (grad_gain_attn, grad_gain_query, grad_gain_key, grad_gain_moe, grad_router), "shard"
+        ),
+        "rep",
     )
     return (
         output,

time: 2260 us -> 2170 us (0.960)
  waiting for transfers between devices: 1580 us -> 1490 us
    psum x1, waiting for transfers between devices: 85.6 us -> 0.02 us  [local(): lax.psum((grad_gain_attn, grad_gain_query, grad_gain_key, grad_gain_moe,...]
  transfers between devices with their start and end apart: 10 -> 11, of which waited for: 10 -> 10; matrix products, arithmetic and copies ran while one was open for 12% -> 15% of each run, Pallas kernels for 0% -> 0%
where the time goes in v1:
time: 2170 us
  waiting for transfers between devices  1490 us (69%)
  matrix products  265 us (12%)
  local copies, waits for them, and re-layouts  190 us (9%)
  other arithmetic  125 us (6%)
  blocking collectives  57.4 us (3%)
    psum x1, waiting for transfers between devices, local(): lax.psum(grad_query_w.astype(jnp.bfloat16), 'rep').astype(jnp.float32)  474 us
    all_to_all x1, waiting for transfers between devices, local(): lax.all_to_all(send_rows.reshape(expert_count, CAP, model_width), 'shard'...  197 us
    all_to_all x1, waiting for transfers between devices, local(): lax.all_to_all(grad_send.reshape(expert_count, CAP, model_width), 'shard'...  189 us
    all_to_all x1, waiting for transfers between devices, local(): lax.all_to_all(grad_expert_in, 'shard', split_axis=1, concat_axis=0, tile...  163 us
    reduce_scatter x1, waiting for transfers between devices, local(): lax.psum_scatter(jnp.dot(flat_attended, proj_out, preferred_element_type=...  159 us
    all_to_all x1, waiting for transfers between devices, local(): lax.all_to_all(expert_out, 'shard', split_axis=1, concat_axis=0, tiled=True)  152 us
    all_gather x1, waiting for transfers between devices, local(): branch_rows = lax.all_gather(grad_branch, 'shard', axis=0, tiled=True)  78.5 us
    all_gather x1, waiting for transfers between devices, local(): lax.all_gather(normed_low, 'shard', axis=0, tiled=True)  69.1 us
  transfers between devices with their start and end apart: 11, of which 10 were waited for; matrix products, arithmetic and copies ran while one was open for 15% of the time, Pallas kernels for 0%

profile of v1, /device:TPU:0, one launch (start us, length us, event | category | flops | bytes accessed | tf_op | source)
XLA Modules:
  0.0 2168.9 jit_solution(2945911509643692916)
XLA Ops:
  28.4 69.1 %all-gather.4.cloned.1.call-done = bf16[2048,2048]{1,0:T(8,128)(2,1)} async-done(((bf16[256,2048]{1,0:T(8,128)(2,1)}), bf16[2048,2048]{1,0:T(8,128)(2,1)}) %all-gather.4.cloned.1.call-update) | async-done | bytes 8388624 | tf_op jit(solution)/shard_map/all_gather | solution.py:124
  174.2 158.8 %reduce-scatter.3.cloned.1.call-done = f32[256,2048]{1,0:T(8,128)} async-done(((f32[2048,2048]{1,0:T(8,128)}), f32[256,2048]{1,0:T(8,128)}) %reduce-scatter.3.cloned.1.call-update) | async-done | bytes 2097168 | tf_op jit(solution)/shard_map/reduce_scatter | solution.py:140
  339.4 18.5 scatter_custom_fusion.1
  363.4 17.6 scatter_custom_fusion
  381.0 188.8 %all-to-all-done.2 = bf16[16,144,2048]{2,1,0:T(8,128)(2,1)} async-done(((bf16[16,144,2048]{2,1,0:T(8,128)(2,1)}), bf16[16,144,2048]{2,1,0:T(8,128)(2,1)}, u32[]{:S(2)}, u32[]{:S(2)}) %all-to-all-start.2) | async-done | bytes 9437216 | tf_op jit(solution)/shard_map/all_to_all | solution.py:185
  584.3 197.1 %all-to-all-done = bf16[16,144,2048]{2,1,0:T(8,128)(2,1)} async-done(((bf16[16,144,2048]{2,1,0:T(8,128)(2,1)}), bf16[16,144,2048]{2,1,0:T(8,128)(2,1)}, u32[]{:S(2)}, u32[]{:S(2)}) %all-to-all-start) | async-done | bytes 9437216 | tf_op jit(solution)/shard_map/all_to_all | solution.py:156
  790.8 17.2 fusion.76
  822.5 23.1 %multiply_convert_fusion = (bf16[2,1152,1024]{2,1,0:T(8,128)(2,1)}, bf16[2,1152,1024]{2,1,0:T(8,128)(2,1)}, bf16[2,1152,1024]{2,1,0:T(8,128)(2,1)}) fusion(f32[2,1152,1024]{2,1,0:T(8,128)} %fusion.75, f32[2,1152,1024]{2,1,0:T(8,128)} %fusion.76, bf16[2,1152,2048]{2,1,0:T(8,128)(2,1)} %bitcast.161, bf16[2,1024,2048]{2,1,0:T(8,128)(2,1)} %param.30), kind=kOutput, calls=%fused_computation.14 | convolution fusion | flops 9699065856 | bytes 50855936 | tf_op jit(solution)/shard_map/erd,efd->erf/dot_general | solution.py:192
  859.9 27.9 %copy.302 = bf16[2,1152,2048]{2,0,1:T(2,128)(2,1)} copy(bf16[2,1152,2048]{2,1,0:T(8,128)(2,1)S(1)} %convolution_convert_fusion) | data formatting | bytes 18874368 | tf_op jit(solution)/shard_map/convert_element_type | solution.py:170
  893.1 17.5 fusion.77
  910.5 18.6 add_convert_fusion
  929.2 18.2 copy.307
  947.4 152.1 %all-to-all-done.1 = bf16[2,1152,2048]{2,0,1:T(2,128)(2,1)} async-done(((bf16[2,1152,2048]{2,0,1:T(2,128)(2,1)}), bf16[2,1152,2048]{2,0,1:T(2,128)(2,1)}, u32[]{:S(2)}, u32[]{:S(2)}) %all-to-all-start.1) | async-done | bytes 9437216 | tf_op jit(solution)/shard_map/all_to_all | solution.py:171
  1116.6 21.8 %gather_fusion = bf16[2048,2048]{1,0:T(8,128)(2,1)} fusion(bf16[2304,2048]{1,0:T(8,128)(2,1)} %bitcast.158, s32[2048]{0:T(1024)S(1)} %broadcast_clamp_fusion), kind=kCustom, calls=%fused_computation | custom fusion | bytes 16785408 | tf_op jit(solution)/shard_map/gather | solution.py:174
  1148.1 162.8 %all-to-all-done.3 = bf16[2,1152,2048]{2,0,1:T(2,128)(2,1)} async-done(((bf16[2,1152,2048]{2,0,1:T(2,128)(2,1)}), bf16[2,1152,2048]{2,0,1:T(2,128)(2,1)}, u32[]{:S(2)}, u32[]{:S(2)}) %all-to-all-start.3) | async-done | bytes 9437216 | tf_op jit(solution)/shard_map/all_to_all | solution.py:208
  1322.7 21.4 gather_fusion.1
  1365.1 78.5 %all-gather.6.cloned.1.call-done = bf16[2048,2048]{1,0:T(8,128)(2,1)} async-done(((bf16[256,2048]{1,0:T(8,128)(2,1)}), bf16[2048,2048]{1,0:T(8,128)(2,1)}) %all-gather.6.cloned.1.call-update) | async-done | bytes 8388624 | tf_op jit(solution)/shard_map/all_gather | solution.py:227
  1487.5 15.7 add_convert_fusion.1
  1503.2 18.2 convolution_convert_fusion.1
  1521.5 17.2 convolution_convert_fusion.2
  1538.7 15.7 convolution_convert_fusion.3
  1597.5 25.9 %all-reduce.4 = (f32[2048]{0:T(1024)S(1)}, f32[128]{0:T(128)S(1)}, f32[128]{0:T(128)S(1)}, f32[2048]{0:T(1024)S(1)}) all-reduce(f32[2048]{0:T(1024)S(1)} %get-tuple-element.22, f32[128]{0:T(128)S(1)} %get-tuple-element.60, f32[128]{0:T(128)S(1)} %get-tuple-element.18, ...), channel_id=1, replica_groups=mesh['rep'=4,'shard'=8] {'shard'}, use_global_device_ids=true, to_apply=%region_27.28 | all-reduce | flops 4352 | bytes 34816 | tf_op jit(solution)/shard_map/psum | solution.py:278
  1623.5 18.0 all-reduce.5
  1641.5 473.9 %all-reduce.15.cloned.1.call-done = (bf16[2048,256]{1,0:T(8,128)(2,1)}, bf16[2048,256]{1,0:T(8,128)(2,1)}, bf16[2048,256]{1,0:T(8,128)(2,1)}, bf16[256,2048]{1,0...) async-done(((bf16[2048,256]{1,0:T(8,128)(2,1)}, bf16[2048,256]{1,0:T(8,128)(2,1)}, ...) | async-done | bytes 29360144 | tf_op jit(solution)/shard_map/psum | solution.py:269
  (315 shorter events, 359.2 us)
Async XLA Ops:
  7.2 150.2 %copy-start = (bf16[256,2048]{1,0:T(8,128)(2,1)S(1)}, bf16[256,2048]{1,0:T(8,128)(2,1)}, u32[]{:S(2)}) copy-start(bf16[256,2048]{1,0:T(8,128)(2,1)} %param.25) | copy-start | bytes 3145732
  7.2 90.3 %copy-start.32 = (bf16[2048,256]{1,0:T(8,128)(2,1)S(1)}, bf16[2048,256]{1,0:T(8,128)(2,1)}, u32[]{:S(2)}) copy-start(bf16[2048,256]{1,0:T(8,128)(2,1)} %param.23) | copy-start | bytes 3145732
  7.2 90.3 %all-gather.4.cloned.1.call-start = ((), (), s32[]{:S(2)}) async-start(), calls=%async_computation.6 | async-start | bytes 9437184 | tf_op jit(solution)/shard_map/all_gather | solution.py:124
  12.6 320.4 %reduce-scatter.3.cloned.1.call-start = ((), (), s32[]{:S(2)}) async-start(), calls=%async_computation.7 | async-start | bytes 18874368 | tf_op jit(solution)/shard_map/reduce_scatter | solution.py:140
  114.4 33.7 %copy-start.3 = (f32[8,256,2,128]{1,3,2,0:T(8,128)}, f32[8,256,2,128]{1,3,2,0:T(8,128)S(1)}, u32[]{:S(2)}) copy-start(f32[8,256,2,128]{1,3,2,0:T(8,128)S(1)} %copy.292) | copy-start | bytes 6291460
  166.7 166.3 %copy-start.8 = (bf16[256,2048]{1,0:T(8,128)(2,1)S(1)}, bf16[256,2048]{1,0:T(8,128)(2,1)}, u32[]{:S(2)}) copy-start(bf16[256,2048]{1,0:T(8,128)(2,1)} %param.16) | copy-start | bytes 3145732
  172.4 162.5 %copy-start.80 = (f32[256]{0:T(256)}, f32[256]{0:T(256)S(1)}, u32[]{:S(2)}) copy-start(f32[256]{0:T(256)S(1)} %compare_convert_fusion) | copy-start | bytes 3076
  172.7 190.7 %copy-start.62 = (s32[2048,1]{0,1:T(1,128)}, s32[2048,1]{0,1:T(1,128)S(1)}, u32[]{:S(2)}) copy-start(s32[2048,1]{0,1:T(1,128)S(1)} %compare_select_fusion) | copy-start | bytes 24580
  172.7 163.6 %copy-start.57 = (f32[2048]{0:T(1024)S(1)}, f32[2048]{0:T(1024)}, u32[]{:S(2)}) copy-start(f32[2048]{0:T(1024)} %param.26) | copy-start | bytes 24580
  174.2 163.3 %copy-start.38 = (bf16[2048,16]{0,1:T(8,128)(2,1)S(1)}, bf16[2048,16]{0,1:T(8,128)(2,1)}, u32[]{:S(2)}) copy-start(bf16[2048,16]{0,1:T(8,128)(2,1)} %param.27) | copy-start | bytes 196612
  358.0 211.7 %all-to-all-start.2 = ((bf16[16,144,2048]{2,1,0:T(8,128)(2,1)}), bf16[16,144,2048]{2,1,0:T(8,128)(2,1)}, u32[]{:S(2)}, u32[]{:S(2)}) async-start(bf16[16,144,2048]{2,1,0:T(8,128)(2,1)} %bitcast.160), calls=%async_computation.3 | async-start | bytes 18874368 | tf_op jit(solution)/shard_map/all_to_all | solution.py:185
  569.7 211.7 %all-to-all-start = ((bf16[16,144,2048]{2,1,0:T(8,128)(2,1)}), bf16[16,144,2048]{2,1,0:T(8,128)(2,1)}, u32[]{:S(2)}, u32[]{:S(2)}) async-start(bf16[16,144,2048]{2,1,0:T(8,128)(2,1)} %bitcast.159), calls=%async_computation.1 | async-start | bytes 18874368 | tf_op jit(solution)/shard_map/all_to_all | solution.py:156
  887.8 211.6 %all-to-all-start.1 = ((bf16[2,1152,2048]{2,0,1:T(2,128)(2,1)}), bf16[2,1152,2048]{2,0,1:T(2,128)(2,1)}, u32[]{:S(2)}, u32[]{:S(2)}) async-start(bf16[2,1152,2048]{2,0,1:T(2,128)(2,1)} %copy.302), calls=%async_computation.2 | async-start | bytes 18874368 | tf_op jit(solution)/shard_map/all_to_all | solution.py:171
  947.4 157.4 %copy-start.63 = (s32[2048,1]{0,1:T(1,128)S(1)}, s32[2048,1]{0,1:T(1,128)}, u32[]{:S(2)}) copy-start(s32[2048,1]{0,1:T(1,128)} %copy-done.62) | copy-start | bytes 24580
  1099.4 211.4 %all-to-all-start.3 = ((bf16[2,1152,2048]{2,0,1:T(2,128)(2,1)}), bf16[2,1152,2048]{2,0,1:T(2,128)(2,1)}, u32[]{:S(2)}, u32[]{:S(2)}) async-start(bf16[2,1152,2048]{2,0,1:T(2,128)(2,1)} %copy.307), calls=%async_computation.4 | async-start | bytes 18874368 | tf_op jit(solution)/shard_map/all_to_all | solution.py:208
  1104.5 339.0 %all-gather.6.cloned.1.call-start = ((), (), s32[]{:S(2)}) async-start(), calls=%async_computation.8 | async-start | bytes 9437184 | tf_op jit(solution)/shard_map/all_gather | solution.py:227
  1116.6 21.8 %copy-start.11 = (f32[256,2048]{1,0:T(8,128)S(1)}, f32[256,2048]{1,0:T(8,128)}, u32[]{:S(2)}) copy-start(f32[256,2048]{1,0:T(8,128)} %convert_multiply_fusion.8) | copy-start | bytes 6291460
  1116.6 21.8 %copy-start.30 = (f32[256,8]{1,0:T(8,128)S(1)}, f32[256,8]{1,0:T(8,128)}, u32[]{:S(2)}) copy-start(f32[256,8]{1,0:T(8,128)} %copy-done.29) | copy-start | bytes 24580
  1362.5 216.6 %all-reduce.11.cloned.1.call-start = ((), (), s32[]{:S(2)}) async-start(), calls=%async_computation.10 | async-start | bytes 262144 | tf_op jit(solution)/shard_map/psum | solution.py:278
  1365.0 226.4 %reduce-scatter.5.cloned.1.call-start = ((), (), s32[]{:S(2)}) async-start(), calls=%async_computation.9 | async-start | bytes 9437184 | tf_op jit(solution)/shard_map/reduce_scatter | solution.py:255
  1503.2 612.2 %all-reduce.15.cloned.1.call-start = ((), (), s32[]{:S(2)}) async-start(), calls=%async_computation.12 | async-start | bytes 58720256 | tf_op jit(solution)/shard_map/psum | solution.py:269
  1503.2 35.5 %slice-start = ((s8[9437184]{0:T(1024)(128)(4,1)}), s8[4194304]{0:T(1024)(128)(4,1)S(1)}, s32[]{:S(2)}) async-start(s8[9437184]{0:T(1024)(128)(4,1)} %bitcast.166), calls=%async_computation.13 | async-start | bytes 8388608
  1503.2 35.5 %slice-start.1 = ((s8[9437184]{0:T(1024)(128)(4,1)}), s8[4194304]{0:T(1024)(128)(4,1)S(1)}, s32[]{:S(2)}) async-start(s8[9437184]{0:T(1024)(128)(4,1)} %bitcast.166), calls=%async_computation.14 | async-start | bytes 8388608
  1579.0 581.2 %all-reduce.13.cloned.1.call-start = ((), (), s32[]{:S(2)}) async-start(), calls=%async_computation.11 | async-start | bytes 262144 | tf_op jit(solution)/shard_map/psum | solution.py:277
  (74 other events, 414.0 us)
Sparse Core Ops, SparseCore 0:
  12.7 84.7 all-gather.3
  166.1 166.8 reduce-scatter.2
  1362.6 80.8 all-gather.5
  1445.7 52.7 all-reduce.10
  1503.3 88.1 reduce-scatter.4
  1597.9 517.4 all-reduce.14
  2118.2 41.9 all-reduce.12
